TPU v7x, 32 devices: a whole 2x2x4 slice. The times are simulated.
32 devices in a mesh: grp: 2 (over x), tok: 4 (over y, core), feat: 4 (over z).
Axes of the slice: x: 2, y: 2, z: 4, core: 2. Of those that a mesh axis runs over, the one named last changes fastest.
Arguments:
- activations: bfloat16 [4096, 3072], P(('grp', 'tok', 'feat')), parts along dimension 0, may hold values from -6 to 6
- block_lists: int32 [2048, 4], P(('grp', 'tok', 'feat')), parts along dimension 0, may hold values from 0 to 15, as said below
- top_positions: int32 [4096, 64], P(('grp', 'tok', 'feat')), parts along dimension 0, may hold values from 0 to 2047, as said below
- enc_weight: bfloat16 [3072, 8192], P(None, ('tok', 'feat')), may hold values from -0.109375 to 0.109375
- enc_bias: float32 [8192], P(('tok', 'feat')), may hold values from -3 to 3
- dec_weight: bfloat16 [8192, 3072], P(('tok', 'feat')), may hold values from -2.5 to 2.5
- dec_bias: float32 [3072], replicated, may hold values from -6 to 6
Outputs:
- enc_grad: bfloat16 [3072, 16384], P(None, ('grp', 'tok', 'feat')), parts along dimension 1
- dec_grad: bfloat16 [16384, 3072], P(('grp', 'tok', 'feat')), parts along dimension 0
There are 2 independent parts, one for each index of `grp`. A program takes and returns all parts, laid end to end along the dimension named above; an argument that names none is the same for every part. Nothing has to cross between parts.
Inputs may be any that keep to these rules, and one draw needn't show every extreme that they name: `block_lists`: each row block names 4 different feature blocks. In the aligned blocks of 64 rows that one device holds, no feature block is named more than 24 times. In every draw one feature block is named exactly 24 times in every such block of rows. `top_positions`: the 64 entries of a token are distinct.
All inputs are finite; a program needn't handle non-finite values.
Results may differ from a plain program's by a relative error of at most 0.0058.
Values may be sent and summed in bfloat16 or wider, within the bound.
A program may use at most 128 MiB of HBM per device.

v0:
```python
import jax
import jax.numpy as jnp
from jax import lax
from jax.sharding import PartitionSpec as P


def dispatch_rows(send_x, send_rel):
    result = (
        lax.all_to_all(send_x, ("tok", "feat"), split_axis=0, concat_axis=0, tiled=True),
        lax.all_to_all(send_rel, ("tok", "feat"), split_axis=0, concat_axis=0, tiled=True),
    )
    return result


def return_partials(partial_value):
    result = lax.all_to_all(partial_value, ("tok", "feat"), split_axis=0, concat_axis=0, tiled=True)
    return result


def dispatch_errors(send_err):
    result = lax.all_to_all(send_err, ("tok", "feat"), split_axis=0, concat_axis=0, tiled=True)
    return result


def routed_plan(
    activations, block_lists, top_positions, enc_weight, enc_bias, dec_weight, dec_bias
):
    owner_count = lax.axis_size(("tok", "feat"))
    token_count, model_width = activations.shape
    block_rows, active_count = block_lists.shape
    group_rows = token_count // block_rows
    feat_block = enc_weight.shape[1]
    top_count = top_positions.shape[1]
    slot_count = max(2, 3 * token_count * active_count // (2 * group_rows * owner_count))
    per_owner = slot_count * group_rows
    buffer_rows = owner_count * per_owner
    pair_count = block_rows * active_count
    pair_ids = block_lists.reshape(pair_count)
    pair_order = jnp.arange(pair_count, dtype=jnp.int32)
    earlier = (pair_ids[:, None] == pair_ids[None, :]) & (pair_order[None, :] < pair_order[:, None])
    pair_rank = jnp.sum(earlier.astype(jnp.int32), axis=1)
    lane_index = jnp.arange(group_rows, dtype=jnp.int32)
    target = (
        (pair_ids * per_owner + pair_rank * group_rows)[:, None] + lane_index[None, :]
    ).reshape(-1)
    source = ((pair_order // active_count * group_rows)[:, None] + lane_index[None, :]).reshape(-1)
    column = jnp.repeat(pair_order % active_count, group_rows)
    slot_index = jnp.arange(buffer_rows, dtype=jnp.int32)
    hit_bool = slot_index[:, None] == target[None, :]
    hit_float = hit_bool.astype(jnp.float32)
    place_float = jnp.sum(
        hit_float.reshape(buffer_rows, block_rows, active_count, group_rows), axis=2
    ).reshape(buffer_rows, token_count)
    place = place_float.astype(jnp.bfloat16)
    filled = jnp.sum(place_float, axis=1)
    send_x = jnp.dot(place, activations, preferred_element_type=jnp.float32).astype(jnp.bfloat16)
    offsets = top_positions[source] - column[:, None] * feat_block
    offsets = jnp.where((offsets >= 0) & (offsets < feat_block), offsets, feat_block)
    rel_float = (
        jnp.dot(hit_float, offsets.astype(jnp.float32), precision=lax.Precision.HIGHEST)
        + (1.0 - filled)[:, None] * feat_block
    )
    send_rel = rel_float.astype(jnp.int32)
    recv_x, recv_rel = dispatch_rows(
        send_x.reshape(owner_count, per_owner, model_width),
        send_rel.reshape(owner_count, per_owner, top_count),
    )
    recv_x = recv_x.reshape(buffer_rows, model_width)
    recv_rel = recv_rel.reshape(buffer_rows, top_count)
    feature_iota = jnp.arange(feat_block, dtype=jnp.int32)
    mask_bool = jnp.zeros((buffer_rows, feat_block), jnp.bool_)
    for begin in range(0, top_count, 8):
        piece = recv_rel[:, begin : begin + 8]
        mask_bool = mask_bool | jnp.any(piece[:, :, None] == feature_iota[None, None, :], axis=1)
    feat_mask = mask_bool.astype(jnp.float32)
    pre_acts = jnp.dot(recv_x, enc_weight, preferred_element_type=jnp.float32) + enc_bias
    code_vals = (feat_mask * pre_acts).astype(jnp.bfloat16)
    partial_value = jnp.dot(code_vals, dec_weight, preferred_element_type=jnp.float32).astype(
        jnp.bfloat16
    )
    returned = return_partials(partial_value.reshape(owner_count, per_owner, model_width)).reshape(
        buffer_rows, model_width
    )
    summed = lax.dot_general(
        place, returned, (((0,), (0,)), ((), ())), preferred_element_type=jnp.float32
    )
    residual = (summed + dec_bias - activations.astype(jnp.float32)).astype(jnp.bfloat16)
    send_err = jnp.dot(place, residual, preferred_element_type=jnp.float32).astype(jnp.bfloat16)
    recv_err = dispatch_errors(send_err.reshape(owner_count, per_owner, model_width)).reshape(
        buffer_rows, model_width
    )
    grad_codes = lax.dot_general(
        recv_err, dec_weight, (((1,), (1,)), ((), ())), preferred_element_type=jnp.float32
    )
    grad_pre = (feat_mask * grad_codes).astype(jnp.bfloat16)
    enc_grad = lax.dot_general(
        recv_x, grad_pre, (((0,), (0,)), ((), ())), preferred_element_type=jnp.float32
    ).astype(jnp.bfloat16)
    raw_grad = lax.dot_general(
        code_vals, recv_err, (((0,), (0,)), ((), ())), preferred_element_type=jnp.float32
    )
    dec_float = dec_weight.astype(jnp.float32)
    along_coef = jnp.sum(raw_grad * dec_float, axis=1) / (
        jnp.sum(dec_float * dec_float, axis=1) + 1e-06
    )
    dec_grad = (raw_grad - along_coef[:, None] * dec_float).astype(jnp.bfloat16)
    return (enc_grad, dec_grad)


GROUP = ("tok", "feat")


def global_ids(block_lists, top_positions, feat_block):
    token_count = top_positions.shape[0]
    block_rows, active_count = block_lists.shape
    lists = jnp.repeat(block_lists, token_count // block_rows, axis=0)
    column = top_positions // feat_block
    chosen = jnp.zeros_like(top_positions)
    for k in range(active_count):
        chosen = jnp.where(column == k, lists[:, k : k + 1], chosen)
    return chosen * feat_block + top_positions % feat_block


def select_mask(rel, feat_block):
    words = feat_block // 8
    inside = (rel >= 0) & (rel < feat_block)
    word = jnp.where(inside, rel // 8, words)
    bit = jnp.left_shift(1, rel & 7)
    word_iota = jnp.arange(words, dtype=jnp.int32)
    packed = jnp.sum(
        jnp.where(word[:, :, None] == word_iota[None, None, :], bit[:, :, None], 0), axis=1
    )
    feature_iota = jnp.arange(feat_block, dtype=jnp.int32)
    spread = (word_iota[:, None] == (feature_iota // 8)[None, :]).astype(jnp.bfloat16)
    wide = jnp.dot(
        packed.astype(jnp.float32).astype(jnp.bfloat16), spread, preferred_element_type=jnp.float32
    ).astype(jnp.int32)
    return (jnp.right_shift(wide, (feature_iota & 7)[None, :]) & 1).astype(jnp.bfloat16)


def gathered_plan(
    activations, block_lists, top_positions, enc_weight, enc_bias, dec_weight, dec_bias
):
    feat_block = enc_weight.shape[1]
    ids = global_ids(block_lists, top_positions, feat_block)
    all_ids = lax.all_gather(ids, GROUP, axis=0, tiled=True)
    all_x = lax.all_gather(activations, GROUP, axis=0, tiled=True)
    mask = select_mask(all_ids - lax.axis_index(GROUP) * feat_block, feat_block)
    pre_acts = jnp.dot(all_x, enc_weight, preferred_element_type=jnp.float32) + enc_bias
    code_vals = jnp.where(mask > 0, pre_acts, 0.0).astype(jnp.bfloat16)
    partial_value = jnp.dot(code_vals, dec_weight, preferred_element_type=jnp.float32).astype(
        jnp.bfloat16
    )
    summed = lax.psum_scatter(partial_value, GROUP, scatter_dimension=0, tiled=True)
    residual = (summed.astype(jnp.float32) + dec_bias - activations.astype(jnp.float32)).astype(
        jnp.bfloat16
    )
    all_err = lax.all_gather(residual, GROUP, axis=0, tiled=True)
    grad_codes = lax.dot_general(
        all_err, dec_weight, (((1,), (1,)), ((), ())), preferred_element_type=jnp.float32
    )
    grad_pre = jnp.where(mask > 0, grad_codes, 0.0).astype(jnp.bfloat16)
    enc_grad = lax.dot_general(
        all_x, grad_pre, (((0,), (0,)), ((), ())), preferred_element_type=jnp.float32
    ).astype(jnp.bfloat16)
    raw_grad = lax.dot_general(
        code_vals, all_err, (((0,), (0,)), ((), ())), preferred_element_type=jnp.float32
    )
    dec_float = dec_weight.astype(jnp.float32)
    along_coef = jnp.sum(raw_grad * dec_float, axis=1) / (
        jnp.sum(dec_float * dec_float, axis=1) + 1e-06
    )
    dec_grad = (raw_grad - along_coef[:, None] * dec_float).astype(jnp.bfloat16)
    return (enc_grad, dec_grad)


def on_device(activations, block_lists, top_positions, *weights):
    owner_count = lax.axis_size(GROUP)
    pairs = activations.shape[0] * block_lists.shape[1]
    gathered = owner_count * activations.shape[0]
    if gathered <= 4 * pairs:
        return gathered_plan(activations, block_lists, top_positions, *weights)
    return routed_plan(activations, block_lists, top_positions, *weights)


def solution(mesh):
    placed = (
        P(("grp", "tok", "feat"), None),
        P(("grp", "tok", "feat"), None),
        P(("grp", "tok", "feat"), None),
        P(None, ("tok", "feat")),
        P(("tok", "feat")),
        P(("tok", "feat"), None),
        P(),
    )
    return jax.shard_map(
        on_device,
        mesh=mesh,
        in_specs=placed,
        out_specs=(P(None, ("grp", "tok", "feat")), P(("grp", "tok", "feat"), None)),
        check_vma=False,
    )
```

profile of v0, /device:TPU:0, one launch (start us, length us, event | category | flops | bytes accessed | tf_op | source)
XLA Modules:
  0.0 425.1 jit_solution(17819520309938272814)
XLA Ops:
  7.2 0.0 copy-start
  7.2 0.0 all-gather.3.cloned.1.call-start
  7.2 0.7 all-gather.3.cloned.1.call-update
  7.9 0.0 reduce-scatter.2.cloned.1.call-start
  8.0 0.9 copy.20
  8.9 0.2 slice_reduce_fusion.3
  9.2 0.8 fusion.11
  10.0 45.2 %all_gather.9 = s32[2048,64]{0,1:T(8,128)S(1)} all-gather(s32[128,64]{0,1:T(8,128)S(1)} %fusion.11), channel_id=1, replica_groups=mesh['grp'=2,'tok'=4,'feat'=4] {'tok','feat'}, dimensions={0}, use_global_device_ids=true | all-gather | bytes 557056 | tf_op jit(solution)/shard_map/all_gather | solution.py:146
  55.2 0.4 fusion.8
  55.6 8.9 %select_reduce_fusion = s32[2048,64]{0,1:T(8,128)S(1)} fusion(s32[2048,64]{0,1:T(8,128)S(1)} %get-tuple-element.17, s32[2048,64]{0,1:T(8,128)S(1)} %get-tuple-element.16), kind=kLoop, calls=%fused_computation | loop fusion | flops 25034752 | bytes 1572864 | tf_op jit(solution)/shard_map/reduce_sum | solution.py:130
  64.5 0.0 copy-start.6
  64.6 2.5 fusion.5
  67.0 54.2 %all-gather.3.cloned.1.call-done = bf16[2048,3072]{1,0:T(8,128)(2,1)} async-done(((bf16[128,3072]{1,0:T(8,128)(2,1)}), bf16[2048,3072]{1,0:T(8,128)(2,1)}) %all-gather.3.cloned.1.call-update) | async-done | bytes 12582928 | tf_op jit(solution)/shard_map/all_gather | solution.py:147
  121.2 0.0 copy-done
  121.2 10.1 %select_convert_fusion.1 = bf16[2048,512]{1,0:T(8,128)(2,1)S(1)} fusion(pred[2048,512]{1,0:T(32,128)(4,1)} %fusion.5, bf16[2048,3072]{1,0:T(8,128)(2,1)} %all-gather.3.cloned.1.call-done, bf16[3072,512]{1,0:T(8,128)(2,1)S(1)} %copy-done, f32[512]{0:T(512)S(1)} %copy-done.6), kind=kOutput, calls=%fused_computation.12 | convolution fusion | flops 6445596672 | bytes 18876416 | tf_op jit(solution)/shard_map/dot_general | solution.py:149
  131.3 0.0 copy-start.7
  131.3 1.3 copy-done.7
  132.6 0.0 copy-done.3
  132.6 9.7 %convolution_convert_fusion = bf16[2048,3072]{1,0:T(8,128)(2,1)} fusion(bf16[2048,512]{1,0:T(8,128)(2,1)S(1)} %select_convert_fusion.1, bf16[512,3072]{1,0:T(8,128)(2,1)S(1)} %copy-done.3), kind=kOutput, calls=%fused_computation.2 | convolution fusion | flops 6448742400 | bytes 17825792 | tf_op jit(solution)/shard_map/dot_general | solution.py:151
  142.4 0.0 reduce-scatter.2.cloned.1.call-update
  142.4 0.0 all-gather.5.cloned.1.call-start
  142.5 133.0 %reduce-scatter.2.cloned.1.call-done = bf16[128,3072]{1,0:T(8,128)(2,1)} async-done(((bf16[2048,3072]{1,0:T(8,128)(2,1)}), bf16[128,3072]{1,0:T(8,128)(2,1)}) %reduce-scatter.2.cloned.1.call-update) | async-done | bytes 786448 | tf_op jit(solution)/shard_map/reduce_scatter | solution.py:154
  275.5 0.0 copy-done.5
  275.5 2.3 subtract_convert_fusion
  277.8 0.0 all-gather.5.cloned.1.call-update
  277.8 100.1 %all-gather.5.cloned.1.call-done = bf16[2048,3072]{1,0:T(8,128)(2,1)} async-done(((bf16[128,3072]{1,0:T(8,128)(2,1)}), bf16[2048,3072]{1,0:T(8,128)(2,1)}) %all-gather.5.cloned.1.call-update) | async-done | bytes 12582928 | tf_op jit(solution)/shard_map/all_gather | solution.py:158
  377.9 23.1 %fusion.4 = bf16[3072,512]{0,1:T(8,128)(2,1)S(1)} fusion(bf16[2048,3072]{1,0:T(8,128)(2,1)} %all-gather.3.cloned.1.call-done, pred[2048,512]{1,0:T(32,128)(4,1)} %fusion.5, bf16[2048,3072]{1,0:T(8,128)(2,1)} %all-gather.5.cloned.1.call-done, bf16[512,3072]{1,0:T(8,128)(2,1)} %param.12), kind=kOutput, calls=%fused_computation.14 | convolution fusion | flops 12888571904 | bytes 32505856 | tf_op jit(solution)/shard_map/dot_general | solution.py:163
  401.0 2.8 copy.21
  403.8 11.7 %fusion.1 = (f32[512]{0:T(512)S(1)}, f32[512]{0:T(512)S(1)}, f32[512,3072]{1,0:T(8,128)S(1)}) fusion(bf16[512,3072]{1,0:T(8,128)(2,1)} %param.12, bf16[2048,512]{1,0:T(8,128)(2,1)} %copy-done.7, bf16[2048,3072]{1,0:T(8,128)(2,1)} %all-gather.5.cloned.1.call-done), kind=kOutput, calls=%fused_computation.7 | convolution fusion | flops 6450314240 | bytes 24121344 | tf_op jit(solution)/shard_map/dot_general | solution.py:166
  415.5 0.0 copy-start.1
  415.5 0.0 copy-done.4
  415.5 3.1 fusion.3
  (10 shorter events, 0.0 us)
Async XLA Ops:
  7.2 114.0 %copy-start = (bf16[3072,512]{1,0:T(8,128)(2,1)S(1)}, bf16[3072,512]{1,0:T(8,128)(2,1)}, u32[]{:S(2)}) copy-start(bf16[3072,512]{1,0:T(8,128)(2,1)} %param.10) | copy-start | bytes 9437188
  7.2 114.0 %all-gather.3.cloned.1.call-start = ((), (), s32[]{:S(2)}) async-start(), calls=%async_computation.1 | async-start | bytes 13369344 | tf_op jit(solution)/shard_map/all_gather | solution.py:147
  7.9 267.6 %reduce-scatter.2.cloned.1.call-start = ((), (), s32[]{:S(2)}) async-start(), calls=%async_computation.2 | async-start | bytes 13369344 | tf_op jit(solution)/shard_map/reduce_scatter | solution.py:154
  64.5 56.7 %copy-start.6 = (f32[512]{0:T(512)S(1)}, f32[512]{0:T(512)}, u32[]{:S(2)}) copy-start(f32[512]{0:T(512)} %param.11) | copy-start | bytes 6148
  121.2 11.4 %copy-start.3 = (bf16[512,3072]{1,0:T(8,128)(2,1)S(1)}, bf16[512,3072]{1,0:T(8,128)(2,1)}, u32[]{:S(2)}) copy-start(bf16[512,3072]{1,0:T(8,128)(2,1)} %param.12) | copy-start | bytes 9437188
  131.3 1.3 copy-start.7
  142.4 133.1 %copy-start.2 = (bf16[128,3072]{1,0:T(8,128)(2,1)S(1)}, bf16[128,3072]{1,0:T(8,128)(2,1)}, u32[]{:S(2)}) copy-start(bf16[128,3072]{1,0:T(8,128)(2,1)} %param.7) | copy-start | bytes 2359300
  142.4 133.1 %copy-start.5 = (f32[3072]{0:T(1024)S(1)}, f32[3072]{0:T(1024)}, u32[]{:S(2)}) copy-start(f32[3072]{0:T(1024)} %param.13) | copy-start | bytes 36868
  142.4 235.5 %all-gather.5.cloned.1.call-start = ((), (), s32[]{:S(2)}) async-start(), calls=%async_computation.3 | async-start | bytes 13369344 | tf_op jit(solution)/shard_map/all_gather | solution.py:158
  403.8 11.7 %copy-start.4 = (bf16[512,3072]{1,0:T(8,128)(2,1)S(1)}, bf16[512,3072]{1,0:T(8,128)(2,1)}, u32[]{:S(2)}) copy-start(bf16[512,3072]{1,0:T(8,128)(2,1)} %param.12) | copy-start | bytes 9437188
  415.5 3.1 copy-start.1
Sparse Core Ops, SparseCore 0:
  10.3 110.8 all-gather.2
  142.5 132.9 reduce-scatter.1
  277.9 99.8 all-gather.4
where the time goes:
time: 425 us
  waiting for transfers between devices  288 us (68%)
  matrix products  57.1 us (13%)
  blocking collectives  45.2 us (11%)
  other arithmetic  15.5 us (4%)
  between operations  13.8 us (3%)
  local copies, waits for them, and re-layouts  5.31 us (1%)
    reduce_scatter x1, waiting for transfers between devices, gathered_plan(): lax.psum_scatter(partial_value, GROUP, scatter_dimension=0, tiled=True)  133 us
    all_gather x1, waiting for transfers between devices, gathered_plan(): all_err = lax.all_gather(residual, GROUP, axis=0, tiled=True)  100 us
    all_gather x1, waiting for transfers between devices, gathered_plan(): all_x = lax.all_gather(activations, GROUP, axis=0, tiled=True)  54.2 us
    all_gather x1, blocking collectives, gathered_plan(): all_ids = lax.all_gather(ids, GROUP, axis=0, tiled=True)  45.2 us
    dot_general x1, matrix products, gathered_plan(): lax.dot_general(all_x, grad_pre, (((0,), (0,)), ((), ())), preferred_elem...  23.1 us
    dot_general x1, matrix products, gathered_plan(): lax.dot_general(code_vals, all_err, (((0,), (0,)), ((), ())), preferred_e...  11.7 us
    dot_general x1, matrix products, gathered_plan(): jnp.dot(all_x, enc_weight, preferred_element_type=jnp.float32) + enc_bias  10.1 us
    dot_general x1, matrix products, gathered_plan(): jnp.dot(code_vals, dec_weight, preferred_element_type=jnp.float32)  9.73 us
  transfers between devices with their start and end apart: 3, of which 3 were waited for; matrix products, arithmetic and copies ran while one was open for 3% of the time, Pallas kernels for 0%

commit v1 on v0

--- a/solution.py
+++ b/solution.py
@@ -2,6 +2,28 @@
 import jax.numpy as jnp
 from jax import lax
 from jax.sharding import PartitionSpec as P
+
+
+def in_order(blocks, dim):
+    shape = list(blocks.shape[1:])
+    shape[dim] *= blocks.shape[0]
+    return jnp.moveaxis(blocks, 0, dim).reshape(shape)
+
+
+def gather_around(x, axis, dim):
+    size = lax.axis_size(axis)
+    pairs = [(i, (i + 1) % size) for i in range(size)]
+    back = [(b, a) for a, b in pairs]
+    lower, upper = ([], [])
+    for step in range(size - 1):
+        if step % 2 == 0:
+            lower.append(lax.ppermute(lower[-1] if lower else x, axis, pairs))
+        else:
+            upper.append(lax.ppermute(upper[-1] if upper else x, axis, back))
+    tiles = jnp.stack([*lower[::-1], x, *upper])
+    shift = lax.axis_index(axis) - len(lower)
+    tiles = tiles[(jnp.arange(size) - shift) % size]
+    return in_order(tiles, dim)
 
 
 def dispatch_rows(send_x, send_rel):
@@ -144,7 +166,7 @@
     feat_block = enc_weight.shape[1]
     ids = global_ids(block_lists, top_positions, feat_block)
     all_ids = lax.all_gather(ids, GROUP, axis=0, tiled=True)
-    all_x = lax.all_gather(activations, GROUP, axis=0, tiled=True)
+    all_x = gather_around(activations, GROUP, 0)
     mask = select_mask(all_ids - lax.axis_index(GROUP) * feat_block, feat_block)
     pre_acts = jnp.dot(all_x, enc_weight, preferred_element_type=jnp.float32) + enc_bias
     code_vals = jnp.where(mask > 0, pre_acts, 0.0).astype(jnp.bfloat16)

time: 425 us -> 631 us (1.48)
  waiting for transfers between devices: 288 us -> 418 us
  local copies, waits for them, and re-layouts: 5.31 us -> 40.3 us
  starting transfers between devices: 0.12 us -> 18.2 us
  blocking collectives: 45.2 us -> 60.7 us
    ppermute x0 -> x15, waiting for transfers between devices: none -> 183 us  [the longest x8 114 us: gather_around(): lower.append(lax.ppermute(lower[-1] if lower else x, axis, pairs))]
    all_gather x1 -> x0, waiting for transfers between devices: 54.2 us -> none  [gathered_plan(): all_x = lax.all_gather(activations, GROUP, axis=0, tiled=True)]
    unnamed x18 -> x58, local copies, waits for them, and re-layouts: 5.06 us -> 28 us
    ppermute x0 -> x15, starting transfers between devices: none -> 18.1 us  [the longest x7 13.7 us: gather_around(): upper.append(lax.ppermute(upper[-1] if upper else x, axis, back))]
    all_gather x1, blocking collectives: 45.2 us -> 60.7 us  [gathered_plan(): all_ids = lax.all_gather(ids, GROUP, axis=0, tiled=True)]
    gather x0 -> x1, local copies, waits for them, and re-layouts: none -> 11.1 us  [gather_around(): tiles = tiles[(jnp.arange(size) - shift) % size]]
  transfers between devices with their start and end apart: 3 -> 17, of which waited for: 3 -> 14; matrix products, arithmetic and copies ran while one was open for 3% -> 6% of each run, Pallas kernels for 0% -> 0%
where the time goes in v1:
time: 631 us; the launch traced here: 628 us
  waiting for transfers between devices  418 us (66%)
  blocking collectives  60.7 us (10%)
  matrix products  60.1 us (10%)
  local copies, waits for them, and re-layouts  40.3 us (6%)
  starting transfers between devices  18.2 us (3%)
  other arithmetic  16.3 us (3%)
  between operations  14.4 us (2%)
    reduce_scatter x1, waiting for transfers between devices, gathered_plan(): lax.psum_scatter(partial_value, GROUP, scatter_dimension=0, tiled=True)  135 us
    ppermute x8, waiting for transfers between devices, gather_around(): lower.append(lax.ppermute(lower[-1] if lower else x, axis, pairs))  114 us
    all_gather x1, waiting for transfers between devices, gathered_plan(): all_err = lax.all_gather(residual, GROUP, axis=0, tiled=True)  101 us
    ppermute x7, waiting for transfers between devices, gather_around(): upper.append(lax.ppermute(upper[-1] if upper else x, axis, back))  68.6 us
    all_gather x1, blocking collectives, gathered_plan(): all_ids = lax.all_gather(ids, GROUP, axis=0, tiled=True)  60.7 us
    unnamed x58, local copies, waits for them, and re-layouts  28 us
    dot_general x1, matrix products, gathered_plan(): lax.dot_general(all_x, grad_pre, (((0,), (0,)), ((), ())), preferred_elem...  25 us
    ppermute x7, starting transfers between devices, gather_around(): upper.append(lax.ppermute(upper[-1] if upper else x, axis, back))  13.7 us
  transfers between devices with their start and end apart: 17, of which 14 were waited for; matrix products, arithmetic and copies ran while one was open for 6% of the time, Pallas kernels for 0%

profile of v1, /device:TPU:0, one launch (start us, length us, event | category | flops | bytes accessed | tf_op | source)
XLA Modules:
  0.0 628.2 jit_solution(17576451533079092559)
XLA Ops:
  7.2 3.1 collective-permute-start
  10.3 19.9 %collective-permute-done = bf16[128,3072]{1,0:T(8,128)(2,1)S(1)} collective-permute-done((bf16[128,3072]{1,0:T(8,128)(2,1)}, bf16[128,3072]{1,0:T(8,128)(2,1)S(1)}, u32[]{:S(2)}, u32[]{:S(2)}) %collective-permute-start) | collective-permute-done | bytes 786464 | tf_op jit(solution)/shard_map/ppermute | solution.py:20
  31.1 4.4 collective-permute-start.8
  35.6 18.0 %collective-permute-done.1 = bf16[128,3072]{1,0:T(8,128)(2,1)S(1)} collective-permute-done((bf16[128,3072]{1,0:T(8,128)(2,1)S(1)}, bf16[128,3072]{1,0:T(8,128)(2,1)S(1)}, u32[]{:S(2)}, u32[]{:S(2)}) %collective-permute-start.1) | collective-permute-done | bytes 786464 | tf_op jit(solution)/shard_map/ppermute | solution.py:20
  53.6 14.2 %collective-permute-done.8 = bf16[128,3072]{1,0:T(8,128)(2,1)S(1)} collective-permute-done((bf16[128,3072]{1,0:T(8,128)(2,1)}, bf16[128,3072]{1,0:T(8,128)(2,1)S(1)}, u32[]{:S(2)}, u32[]{:S(2)}) %collective-permute-start.8) | collective-permute-done | bytes 786464 | tf_op jit(solution)/shard_map/ppermute | solution.py:22
  68.6 2.8 collective-permute-start.9
  71.4 16.0 %collective-permute-done.2 = bf16[128,3072]{1,0:T(8,128)(2,1)S(1)} collective-permute-done((bf16[128,3072]{1,0:T(8,128)(2,1)S(1)}, bf16[128,3072]{1,0:T(8,128)(2,1)S(1)}, u32[]{:S(2)}, u32[]{:S(2)}) %collective-permute-start.2) | collective-permute-done | bytes 786464 | tf_op jit(solution)/shard_map/ppermute | solution.py:20
  87.4 16.8 %collective-permute-done.9 = bf16[128,3072]{1,0:T(8,128)(2,1)S(1)} collective-permute-done((bf16[128,3072]{1,0:T(8,128)(2,1)S(1)}, bf16[128,3072]{1,0:T(8,128)(2,1)S(1)}, u32[]{:S(2)}, u32[]{:S(2)}) %collective-permute-start.9) | collective-permute-done | bytes 786464 | tf_op jit(solution)/shard_map/ppermute | solution.py:22
  105.1 16.1 %collective-permute-done.3 = bf16[128,3072]{1,0:T(8,128)(2,1)S(1)} collective-permute-done((bf16[128,3072]{1,0:T(8,128)(2,1)S(1)}, bf16[128,3072]{1,0:T(8,128)(2,1)S(1)}, u32[]{:S(2)}, u32[]{:S(2)}) %collective-permute-start.3) | collective-permute-done | bytes 786464 | tf_op jit(solution)/shard_map/ppermute | solution.py:20
  121.1 17.7 %collective-permute-done.10 = bf16[128,3072]{1,0:T(8,128)(2,1)} collective-permute-done((bf16[128,3072]{1,0:T(8,128)(2,1)S(1)}, bf16[128,3072]{1,0:T(8,128)(2,1)}, u32[]{:S(2)}, u32[]{:S(2)}) %collective-permute-start.10) | collective-permute-done | bytes 786464 | tf_op jit(solution)/shard_map/ppermute | solution.py:22
  138.8 16.2 %collective-permute-done.4 = bf16[128,3072]{1,0:T(8,128)(2,1)} collective-permute-done((bf16[128,3072]{1,0:T(8,128)(2,1)S(1)}, bf16[128,3072]{1,0:T(8,128)(2,1)}, u32[]{:S(2)}, u32[]{:S(2)}) %collective-permute-start.4) | collective-permute-done | bytes 786464 | tf_op jit(solution)/shard_map/ppermute | solution.py:20
  156.0 16.5 %collective-permute-done.11 = bf16[128,3072]{1,0:T(8,128)(2,1)} collective-permute-done((bf16[128,3072]{1,0:T(8,128)(2,1)}, bf16[128,3072]{1,0:T(8,128)(2,1)}, u32[]{:S(2)}, u32[]{:S(2)}) %collective-permute-start.11) | collective-permute-done | bytes 786464 | tf_op jit(solution)/shard_map/ppermute | solution.py:22
  172.5 16.2 %collective-permute-done.5 = bf16[128,3072]{1,0:T(8,128)(2,1)} collective-permute-done((bf16[128,3072]{1,0:T(8,128)(2,1)}, bf16[128,3072]{1,0:T(8,128)(2,1)}, u32[]{:S(2)}, u32[]{:S(2)}) %collective-permute-start.5) | collective-permute-done | bytes 786464 | tf_op jit(solution)/shard_map/ppermute | solution.py:20
  189.5 60.7 %all_gather.6 = s32[2048,64]{0,1:T(8,128)S(1)} all-gather(s32[128,64]{0,1:T(8,128)S(1)} %fusion.10), channel_id=1, replica_groups=mesh['grp'=2,'tok'=4,'feat'=4] {'tok','feat'}, dimensions={0}, use_global_device_ids=true | all-gather | bytes 557056 | tf_op jit(solution)/shard_map/all_gather | solution.py:168
  253.2 9.7 %select_reduce_fusion = s32[2048,64]{0,1:T(8,128)} fusion(s32[2048,64]{0,1:T(8,128)S(1)} %get-tuple-element.9, s32[2048,64]{0,1:T(8,128)S(1)} %get-tuple-element.8), kind=kLoop, calls=%fused_computation.1 | loop fusion | flops 25034752 | bytes 1572864 | tf_op jit(solution)/shard_map/reduce_sum | solution.py:152
  263.0 3.7 fusion.4
  266.7 3.4 collective-permute-done.13
  270.2 5.1 collective-permute-start.14
  275.3 11.7 %collective-permute-done.7 = bf16[128,3072]{1,0:T(8,128)(2,1)} collective-permute-done((bf16[128,3072]{1,0:T(8,128)(2,1)}, bf16[128,3072]{1,0:T(8,128)(2,1)}, u32[]{:S(2)}, u32[]{:S(2)}) %collective-permute-start.7) | collective-permute-done | bytes 786464 | tf_op jit(solution)/shard_map/ppermute | solution.py:20
  287.0 2.1 bitcast_dynamic-update-slice_fusion.15
  291.2 2.1 bitcast_dynamic-update-slice_fusion.13
  293.3 2.1 bitcast_dynamic-update-slice_fusion.12
  302.0 2.1 bitcast_dynamic-update-slice_fusion.4
  311.4 11.1 %gather_fusion = bf16[16,128,3072]{2,1,0:T(8,128)(2,1)} fusion(bf16[16,128,3072]{2,1,0:T(8,128)(2,1)} %bitcast_dynamic-update-slice_fusion, s32[1024]{0:T(1024)S(1)} %pad_clamp_fusion), kind=kCustom, calls=%fused_computation | custom fusion | bytes 25165888 | tf_op jit(solution)/shard_map/gather | solution.py:25
  322.4 10.0 %select_convert_fusion.1 = bf16[2048,512]{1,0:T(8,128)(2,1)S(1)} fusion(pred[2048,512]{1,0:T(32,128)(4,1)} %fusion.4, bf16[2048,3072]{1,0:T(8,128)(2,1)} %bitcast.45, bf16[3072,512]{1,0:T(8,128)(2,1)S(1)} %copy-done, f32[512]{0:T(512)S(1)} %copy-done.19), kind=kOutput, calls=%fused_computation.13 | convolution fusion | flops 6445596672 | bytes 18876416 | tf_op jit(solution)/shard_map/dot_general | solution.py:171
  333.7 9.6 %convolution_convert_fusion = bf16[2048,3072]{1,0:T(8,128)(2,1)} fusion(bf16[2048,512]{1,0:T(8,128)(2,1)S(1)} %select_convert_fusion.1, bf16[512,3072]{1,0:T(8,128)(2,1)S(1)} %copy-done.4), kind=kOutput, calls=%fused_computation.3 | convolution fusion | flops 6448742400 | bytes 17825792 | tf_op jit(solution)/shard_map/dot_general | solution.py:173
  343.4 135.0 %reduce-scatter.2.cloned.1.call-done = bf16[128,3072]{1,0:T(8,128)(2,1)} async-done(((bf16[2048,3072]{1,0:T(8,128)(2,1)}), bf16[128,3072]{1,0:T(8,128)(2,1)}) %reduce-scatter.2.cloned.1.call-update) | async-done | bytes 786448 | tf_op jit(solution)/shard_map/reduce_scatter | solution.py:176
  478.5 2.3 subtract_convert_fusion
  480.7 100.6 %all-gather.2.cloned.1.call-done = bf16[2048,3072]{1,0:T(8,128)(2,1)} async-done(((bf16[128,3072]{1,0:T(8,128)(2,1)}), bf16[2048,3072]{1,0:T(8,128)(2,1)}) %all-gather.2.cloned.1.call-update) | async-done | bytes 12582928 | tf_op jit(solution)/shard_map/all_gather | solution.py:180
  581.3 11.8 %fusion.1 = (f32[512]{0:T(512)S(1)}, f32[512]{0:T(512)S(1)}, f32[512,3072]{1,0:T(8,128)S(1)}) fusion(bf16[512,3072]{1,0:T(8,128)(2,1)} %param.12, bf16[2048,512]{1,0:T(8,128)(2,1)} %copy-done.20, bf16[2048,3072]{1,0:T(8,128)(2,1)} %all-gather.2.cloned.1.call-done), kind=kOutput, calls=%fused_computation.8 | convolution fusion | flops 6450314240 | bytes 24121344 | tf_op jit(solution)/shard_map/dot_general | solution.py:188
  593.1 3.1 fusion.3
  596.2 25.0 %convolution_convert_fusion.1 = bf16[3072,512]{1,0:T(8,128)(2,1)} fusion(bf16[2048,3072]{1,0:T(8,128)(2,1)} %bitcast.46, pred[2048,512]{1,0:T(32,128)(4,1)} %fusion.4, bf16[2048,3072]{1,0:T(8,128)(2,1)} %all-gather.2.cloned.1.call-done, bf16[512,3072]{1,0:T(8,128)(2,1)} %param.12), kind=kOutput, calls=%fused_computation.11 | convolution fusion | flops 12888571904 | bytes 32505856 | tf_op jit(solution)/shard_map/dot_general | solution.py:185
  (81 shorter events, 24.9 us)
Async XLA Ops:
  7.2 315.3 %copy-start = (bf16[3072,512]{1,0:T(8,128)(2,1)S(1)}, bf16[3072,512]{1,0:T(8,128)(2,1)}, u32[]{:S(2)}) copy-start(bf16[3072,512]{1,0:T(8,128)(2,1)} %param.10) | copy-start | bytes 9437188
  7.2 471.3 %reduce-scatter.2.cloned.1.call-start = ((), (), s32[]{:S(2)}) async-start(), calls=%async_computation.1 | async-start | bytes 13369344 | tf_op jit(solution)/shard_map/reduce_scatter | solution.py:176
  7.2 23.0 %collective-permute-start = (bf16[128,3072]{1,0:T(8,128)(2,1)}, bf16[128,3072]{1,0:T(8,128)(2,1)S(1)}, u32[]{:S(2)}, u32[]{:S(2)}) collective-permute-start(bf16[128,3072]{1,0:T(8,128)(2,1)} %param.7), channel_id=1, source_target_pairs={{0,1},{1,2},{2,3},{3,4},{4,5},{5,6},{6,7},{7,8},{8,9},{9,10},{10,1... | collective-permute-start | bytes 2359304 | tf_op jit(solution)/shard_map/ppermute | solution.py:20
  31.1 22.5 %collective-permute-start.1 = (bf16[128,3072]{1,0:T(8,128)(2,1)S(1)}, bf16[128,3072]{1,0:T(8,128)(2,1)S(1)}, u32[]{:S(2)}, u32[]{:S(2)}) collective-permute-start(bf16[128,3072]{1,0:T(8,128)(2,1)S(1)} %collective-permute-done), channel_id=1, source_target_pairs={{0,1},{1,2},{2,3},{3,4},{4,5},{5,6},{6,7},{7,8},{8,9},{9,10},{10,1... | collective-permute-start | bytes 2359304 | tf_op jit(solution)/shard_map/ppermute | solution.py:20
  31.1 36.6 %collective-permute-start.8 = (bf16[128,3072]{1,0:T(8,128)(2,1)}, bf16[128,3072]{1,0:T(8,128)(2,1)S(1)}, u32[]{:S(2)}, u32[]{:S(2)}) collective-permute-start(bf16[128,3072]{1,0:T(8,128)(2,1)} %param.7), channel_id=1, source_target_pairs={{1,0},{2,1},{3,2},{4,3},{5,4},{6,5},{7,6},{8,7},{9,8},{10,9},{11,1... | collective-permute-start | bytes 2359304 | tf_op jit(solution)/shard_map/ppermute | solution.py:22
  53.6 50.6 %copy-start.10 = (bf16[128,3072]{1,0:T(8,128)(2,1)}, bf16[128,3072]{1,0:T(8,128)(2,1)S(1)}, u32[]{:S(2)}) copy-start(bf16[128,3072]{1,0:T(8,128)(2,1)S(1)} %collective-permute-done.1) | copy-start | bytes 2359300
  53.6 33.8 %collective-permute-start.2 = (bf16[128,3072]{1,0:T(8,128)(2,1)S(1)}, bf16[128,3072]{1,0:T(8,128)(2,1)S(1)}, u32[]{:S(2)}, u32[]{:S(2)}) collective-permute-start(bf16[128,3072]{1,0:T(8,128)(2,1)S(1)} %collective-permute-done.1), channel_id=1, source_target_pairs={{0,1},{1,2},{2,3},{3,4},{4,5},{5,6},{6,7},{7,8},{8,9},{9,10},{10,1... | collective-permute-start | bytes 2359304 | tf_op jit(solution)/shard_map/ppermute | solution.py:20
  68.6 35.5 %collective-permute-start.9 = (bf16[128,3072]{1,0:T(8,128)(2,1)S(1)}, bf16[128,3072]{1,0:T(8,128)(2,1)S(1)}, u32[]{:S(2)}, u32[]{:S(2)}) collective-permute-start(bf16[128,3072]{1,0:T(8,128)(2,1)S(1)} %collective-permute-done.8), channel_id=1, source_target_pairs={{1,0},{2,1},{3,2},{4,3},{5,4},{6,5},{7,6},{8,7},{9,8},{10,9},{11,1... | collective-permute-start | bytes 2359304 | tf_op jit(solution)/shard_map/ppermute | solution.py:22
  87.4 51.4 %copy-start.14 = (bf16[128,3072]{1,0:T(8,128)(2,1)}, bf16[128,3072]{1,0:T(8,128)(2,1)S(1)}, u32[]{:S(2)}) copy-start(bf16[128,3072]{1,0:T(8,128)(2,1)S(1)} %collective-permute-done.2) | copy-start | bytes 2359300
  87.4 33.8 %collective-permute-start.3 = (bf16[128,3072]{1,0:T(8,128)(2,1)S(1)}, bf16[128,3072]{1,0:T(8,128)(2,1)S(1)}, u32[]{:S(2)}, u32[]{:S(2)}) collective-permute-start(bf16[128,3072]{1,0:T(8,128)(2,1)S(1)} %collective-permute-done.2), channel_id=1, source_target_pairs={{0,1},{1,2},{2,3},{3,4},{4,5},{5,6},{6,7},{7,8},{8,9},{9,10},{10,1... | collective-permute-start | bytes 2359304 | tf_op jit(solution)/shard_map/ppermute | solution.py:20
  104.2 34.6 %collective-permute-start.10 = (bf16[128,3072]{1,0:T(8,128)(2,1)S(1)}, bf16[128,3072]{1,0:T(8,128)(2,1)}, u32[]{:S(2)}, u32[]{:S(2)}) collective-permute-start(bf16[128,3072]{1,0:T(8,128)(2,1)S(1)} %collective-permute-done.9), channel_id=1, source_target_pairs={{1,0},{2,1},{3,2},{4,3},{5,4},{6,5},{7,6},{8,7},{9,8},{10,9},{11,1... | collective-permute-start | bytes 2359304 | tf_op jit(solution)/shard_map/ppermute | solution.py:22
  121.1 17.7 %copy-start.16 = (bf16[128,3072]{1,0:T(8,128)(2,1)}, bf16[128,3072]{1,0:T(8,128)(2,1)S(1)}, u32[]{:S(2)}) copy-start(bf16[128,3072]{1,0:T(8,128)(2,1)S(1)} %collective-permute-done.3) | copy-start | bytes 2359300
  121.1 33.9 %collective-permute-start.4 = (bf16[128,3072]{1,0:T(8,128)(2,1)S(1)}, bf16[128,3072]{1,0:T(8,128)(2,1)}, u32[]{:S(2)}, u32[]{:S(2)}) collective-permute-start(bf16[128,3072]{1,0:T(8,128)(2,1)S(1)} %collective-permute-done.3), channel_id=1, source_target_pairs={{0,1},{1,2},{2,3},{3,4},{4,5},{5,6},{6,7},{7,8},{8,9},{9,10},{10,1... | collective-permute-start | bytes 2359304 | tf_op jit(solution)/shard_map/ppermute | solution.py:20
  138.8 33.7 %collective-permute-start.11 = (bf16[128,3072]{1,0:T(8,128)(2,1)}, bf16[128,3072]{1,0:T(8,128)(2,1)}, u32[]{:S(2)}, u32[]{:S(2)}) collective-permute-start(bf16[128,3072]{1,0:T(8,128)(2,1)} %collective-permute-done.10), channel_id=1, source_target_pairs={{1,0},{2,1},{3,2},{4,3},{5,4},{6,5},{7,6},{8,7},{9,8},{10,9},{11,1... | collective-permute-start | bytes 2359304 | tf_op jit(solution)/shard_map/ppermute | solution.py:22
  155.0 33.7 %collective-permute-start.5 = (bf16[128,3072]{1,0:T(8,128)(2,1)}, bf16[128,3072]{1,0:T(8,128)(2,1)}, u32[]{:S(2)}, u32[]{:S(2)}) collective-permute-start(bf16[128,3072]{1,0:T(8,128)(2,1)} %collective-permute-done.4), channel_id=1, source_target_pairs={{0,1},{1,2},{2,3},{3,4},{4,5},{5,6},{6,7},{7,8},{8,9},{9,10},{10,1... | collective-permute-start | bytes 2359304 | tf_op jit(solution)/shard_map/ppermute | solution.py:20
  172.5 78.1 %collective-permute-start.12 = (bf16[128,3072]{1,0:T(8,128)(2,1)}, bf16[128,3072]{1,0:T(8,128)(2,1)}, u32[]{:S(2)}, u32[]{:S(2)}) collective-permute-start(bf16[128,3072]{1,0:T(8,128)(2,1)} %collective-permute-done.11), channel_id=1, source_target_pairs={{1,0},{2,1},{3,2},{4,3},{5,4},{6,5},{7,6},{8,7},{9,8},{10,9},{11,1... | collective-permute-start | bytes 2359304 | tf_op jit(solution)/shard_map/ppermute | solution.py:22
  188.7 63.2 %collective-permute-start.6 = (bf16[128,3072]{1,0:T(8,128)(2,1)}, bf16[128,3072]{1,0:T(8,128)(2,1)}, u32[]{:S(2)}, u32[]{:S(2)}) collective-permute-start(bf16[128,3072]{1,0:T(8,128)(2,1)} %collective-permute-done.5), channel_id=1, source_target_pairs={{0,1},{1,2},{2,3},{3,4},{4,5},{5,6},{6,7},{7,8},{8,9},{9,10},{10,1... | collective-permute-start | bytes 2359304 | tf_op jit(solution)/shard_map/ppermute | solution.py:20
  250.6 19.5 %collective-permute-start.13 = (bf16[128,3072]{1,0:T(8,128)(2,1)}, bf16[128,3072]{1,0:T(8,128)(2,1)}, u32[]{:S(2)}, u32[]{:S(2)}) collective-permute-start(bf16[128,3072]{1,0:T(8,128)(2,1)} %collective-permute-done.12), channel_id=1, source_target_pairs={{1,0},{2,1},{3,2},{4,3},{5,4},{6,5},{7,6},{8,7},{9,8},{10,9},{11,1... | collective-permute-start | bytes 2359304 | tf_op jit(solution)/shard_map/ppermute | solution.py:22
  251.9 35.1 %collective-permute-start.7 = (bf16[128,3072]{1,0:T(8,128)(2,1)}, bf16[128,3072]{1,0:T(8,128)(2,1)}, u32[]{:S(2)}, u32[]{:S(2)}) collective-permute-start(bf16[128,3072]{1,0:T(8,128)(2,1)} %collective-permute-done.6), channel_id=1, source_target_pairs={{0,1},{1,2},{2,3},{3,4},{4,5},{5,6},{6,7},{7,8},{8,9},{9,10},{10,1... | collective-permute-start | bytes 2359304 | tf_op jit(solution)/shard_map/ppermute | solution.py:20
  262.9 32.5 %copy-start.17 = (bf16[128,3072]{1,0:T(8,128)(2,1)S(1)}, bf16[128,3072]{1,0:T(8,128)(2,1)}, u32[]{:S(2)}) copy-start(bf16[128,3072]{1,0:T(8,128)(2,1)} %copy-done.16) | copy-start | bytes 2359300
  262.9 33.4 %copy-start.15 = (bf16[128,3072]{1,0:T(8,128)(2,1)S(1)}, bf16[128,3072]{1,0:T(8,128)(2,1)}, u32[]{:S(2)}) copy-start(bf16[128,3072]{1,0:T(8,128)(2,1)} %copy-done.14) | copy-start | bytes 2359300
  262.9 34.4 %copy-start.11 = (bf16[128,3072]{1,0:T(8,128)(2,1)S(1)}, bf16[128,3072]{1,0:T(8,128)(2,1)}, u32[]{:S(2)}) copy-start(bf16[128,3072]{1,0:T(8,128)(2,1)} %copy-done.10) | copy-start | bytes 2359300
  262.9 35.3 %copy-start.7 = (bf16[128,3072]{1,0:T(8,128)(2,1)S(1)}, bf16[128,3072]{1,0:T(8,128)(2,1)}, u32[]{:S(2)}) copy-start(bf16[128,3072]{1,0:T(8,128)(2,1)} %copy-done.6) | copy-start | bytes 2359300
  262.9 36.3 %copy-start.2 = (bf16[128,3072]{1,0:T(8,128)(2,1)S(1)}, bf16[128,3072]{1,0:T(8,128)(2,1)}, u32[]{:S(2)}) copy-start(bf16[128,3072]{1,0:T(8,128)(2,1)} %param.7) | copy-start | bytes 2359300
  262.9 37.2 %copy-start.9 = (bf16[128,3072]{1,0:T(8,128)(2,1)S(1)}, bf16[128,3072]{1,0:T(8,128)(2,1)}, u32[]{:S(2)}) copy-start(bf16[128,3072]{1,0:T(8,128)(2,1)} %copy-done.8) | copy-start | bytes 2359300
  263.0 38.1 %copy-start.13 = (bf16[128,3072]{1,0:T(8,128)(2,1)S(1)}, bf16[128,3072]{1,0:T(8,128)(2,1)}, u32[]{:S(2)}) copy-start(bf16[128,3072]{1,0:T(8,128)(2,1)} %copy-done.12) | copy-start | bytes 2359300
  270.2 40.2 %collective-permute-start.14 = (bf16[128,3072]{1,0:T(8,128)(2,1)}, bf16[128,3072]{1,0:T(8,128)(2,1)S(1)}, u32[]{:S(2)}, u32[]{:S(2)}) collective-permute-start(bf16[128,3072]{1,0:T(8,128)(2,1)} %collective-permute-done.13), channel_id=1, source_target_pairs={{1,0},{2,1},{3,2},{4,3},{5,4},{6,5},{7,6},{8,7},{9,8},{10,9},{11,1... | collective-permute-start | bytes 2359304 | tf_op jit(solution)/shard_map/ppermute | solution.py:22
  343.3 135.1 %copy-start.3 = (bf16[128,3072]{1,0:T(8,128)(2,1)S(1)}, bf16[128,3072]{1,0:T(8,128)(2,1)}, u32[]{:S(2)}) copy-start(bf16[128,3072]{1,0:T(8,128)(2,1)} %param.7) | copy-start | bytes 2359300
  343.3 135.1 %copy-start.18 = (f32[3072]{0:T(1024)S(1)}, f32[3072]{0:T(1024)}, u32[]{:S(2)}) copy-start(f32[3072]{0:T(1024)} %param.13) | copy-start | bytes 36868
  343.4 237.9 %all-gather.2.cloned.1.call-start = ((), (), s32[]{:S(2)}) async-start(), calls=%async_computation.2 | async-start | bytes 13369344 | tf_op jit(solution)/shard_map/all_gather | solution.py:180
  480.7 112.4 %copy-start.5 = (bf16[512,3072]{1,0:T(8,128)(2,1)S(1)}, bf16[512,3072]{1,0:T(8,128)(2,1)}, u32[]{:S(2)}) copy-start(bf16[512,3072]{1,0:T(8,128)(2,1)} %param.12) | copy-start | bytes 9437188
  596.2 25.0 %copy-start.1 = (bf16[3072,512]{1,0:T(8,128)(2,1)S(1)}, bf16[3072,512]{1,0:T(8,128)(2,1)}, u32[]{:S(2)}) copy-start(bf16[3072,512]{1,0:T(8,128)(2,1)} %param.10) | copy-start | bytes 9437188
  (6 other events, 26.4 us)
Sparse Core Ops, SparseCore 0:
  343.5 134.9 reduce-scatter.1
  481.3 99.9 all-gather.1
